TPU v7x, 256 devices: a whole 4x4x8 slice. The times are simulated.
256 devices in a mesh: batch: 64 (over y, z, core), feat: 4 (over x).
Axes of the slice: x: 4, y: 4, z: 8, core: 2. Of those that a mesh axis runs over, the one named last changes fastest.
Arguments:
- tables: bfloat16 [4, 128, 2048, 192], P('feat', 'batch'), may hold values from -3 to 3
- bag_ids: int32 [4, 128, 4, 8192], P('feat', 'batch'), may hold values from 0 to 2047
- bag_lengths: int32 [4, 128, 8192], P('feat', 'batch'), may hold values from 1 to 4
- pair_groups: int32 [16, 2], replicated, may hold values from 0 to 15
- compress: bfloat16 [16, 32, 8], P('feat'), may hold values from -1 to 1
- w_hidden: bfloat16 [16, 32, 8, 4096], P('feat'), may hold values from -0.09375 to 0.09375
- hidden_bias: float32 [4096], replicated, may hold values from -4 to 4
- norm_gain: float32 [4096], P('feat'), may hold values from 0.1 to 1.9
Outputs:
- interacted: bfloat16 [8192, 4096], P('batch', 'feat')
Inputs may be any that keep to these rules, and one draw needn't show every extreme that they name: `bag_lengths`: ids at slots from a bag's length on are ignored.
All inputs are finite; a program needn't handle non-finite values.
Results may differ from a plain program's by a relative error of at most 0.0052.
Values may be sent and summed in bfloat16 or wider, within the bound.
A program may use at most 128 MiB of HBM per device.

v0:
```python
import jax
import jax.numpy as jnp
from jax import lax
from jax.sharding import PartitionSpec as P


def take_rows(table_one, ids_one):
    return jnp.take(table_one, ids_one, axis=0)


def select_groups(source, pair_list, group_size):
    offsets = jnp.arange(group_size, dtype=jnp.int32)
    wanted = pair_list[:, :, None] * group_size + offsets[None, None, :]
    shape_out = (pair_list.shape[0], 2, group_size, source.shape[1], source.shape[2])
    return jnp.take(source, wanted.reshape(-1), axis=0).reshape(shape_out)


def squeeze_pairs(chosen, weights):
    row_blocks = chosen[:, 0]
    col_blocks = chosen[:, 1]
    gram_scale = float(chosen.shape[4]) ** (-0.5)
    gram_blocks = (
        jnp.einsum("qfbd,qgbd->qbfg", row_blocks, col_blocks, preferred_element_type=jnp.float32)
        * gram_scale
    )
    squeezed = jnp.einsum(
        "qbfg,qgk->bqfk", gram_blocks, weights.astype(jnp.float32), precision=lax.Precision.HIGHEST
    )
    return squeezed.astype(jnp.bfloat16)


def body(tables, bag_ids, bag_lengths, pair_groups, compress, w_hidden, hidden_bias, norm_gain):
    own_tables = tables[0]
    own_ids = bag_ids[0]
    own_lengths = bag_lengths[0]
    slot_count = own_ids.shape[1]
    pooled_sum = jnp.zeros((own_ids.shape[0], own_ids.shape[2], own_tables.shape[2]), jnp.float32)
    for slot in range(slot_count):
        looked = jax.vmap(take_rows)(own_tables, own_ids[:, slot, :])
        live = (own_lengths > slot)[:, :, None]
        pooled_sum = pooled_sum + jnp.where(live, looked.astype(jnp.float32), 0.0)
    pooled = pooled_sum.astype(jnp.bfloat16)
    feature_tile = lax.all_to_all(pooled, "batch", split_axis=1, concat_axis=0, tiled=True)
    samples = feature_tile.shape[1]
    pair_count = compress.shape[0]
    group_size = compress.shape[1]
    first_pair = lax.axis_index("feat") * pair_count
    local_pairs = lax.dynamic_slice_in_dim(pair_groups, first_pair, pair_count, 0)
    everything = lax.all_gather(feature_tile, "feat", axis=0, tiled=True)
    squeezed = squeeze_pairs(select_groups(everything, local_pairs, group_size), compress)
    squeezed = squeezed.reshape(samples, -1)
    w_flat = w_hidden.reshape(-1, w_hidden.shape[3])
    hid_local = norm_gain.shape[0]
    hid_total = hid_local * lax.axis_size("feat")
    own_start = lax.axis_index("feat") * hid_local
    hidden = lax.psum_scatter(
        lax.dot_general(
            w_flat, squeezed, (((0,), (1,)), ((), ())), preferred_element_type=jnp.float32
        ),
        "feat",
        scatter_dimension=0,
        tiled=True,
    )
    local_bias = lax.dynamic_slice_in_dim(hidden_bias, own_start, hid_local, 0)
    hidden = hidden + local_bias[:, None]
    row_sum, row_squares = lax.psum(
        (jnp.sum(hidden, axis=0), jnp.sum(hidden * hidden, axis=0)), "feat"
    )
    row_mean = row_sum / hid_total
    spread = row_squares / hid_total - row_mean * row_mean
    normed = (hidden - row_mean[None, :]) * lax.rsqrt(spread + 1e-05)[None, :] * norm_gain[:, None]
    return jax.nn.silu(normed).T.astype(jnp.bfloat16)


def solution(mesh):
    in_specs = (
        P("feat", "batch", None, None),
        P("feat", "batch", None, None),
        P("feat", "batch", None),
        P(),
        P("feat", None, None),
        P("feat", None, None, None),
        P(),
        P("feat"),
    )
    out_specs = P("batch", "feat")
    return jax.shard_map(body, mesh=mesh, in_specs=in_specs, out_specs=out_specs, check_vma=False)
```

profile of v0, /device:TPU:8, one launch (start us, length us, event | category | flops | bytes accessed | tf_op | source)
XLA Modules:
  0.0 1334.6 jit_solution(744671372483452733)
XLA Ops:
  6.5 0.0 copy-start
  6.5 0.0 all-gather.2.cloned.1.call-start
  6.5 1.8 fusion.15
  8.3 0.2 fusion.12
  8.5 0.2 compare_and_fusion.2
  8.7 0.2 fusion.10
  8.9 0.2 compare_and_fusion
  9.1 2.7 copy.38
  11.9 161.2 %gather_fusion.3 = bf16[16384,192]{1,0:T(8,128)(2,1)} fusion(bf16[2,2048,192]{2,1,0:T(8,128)(2,1)S(1)} %bitcast.104, s32[16384]{0:T(1024)S(1)} %bitcast.108), kind=kCustom, calls=%fused_computation.2.clone | custom fusion | bytes 12713984 | tf_op jit(solution)/shard_map/vmap(jit(_take))/gather | solution.py:8
  173.1 161.2 %gather_fusion.4 = bf16[16384,192]{1,0:T(8,128)(2,1)} fusion(bf16[2,2048,192]{2,1,0:T(8,128)(2,1)S(1)} %bitcast.105, s32[16384]{0:T(1024)S(1)} %bitcast.109), kind=kCustom, calls=%fused_computation.3.clone | custom fusion | bytes 12713984 | tf_op jit(solution)/shard_map/vmap(jit(_take))/gather | solution.py:8
  334.3 161.1 %gather_fusion.1 = bf16[16384,192]{1,0:T(8,128)(2,1)} fusion(bf16[2,2048,192]{2,1,0:T(8,128)(2,1)S(1)} %bitcast.106, s32[16384]{0:T(1024)S(1)} %bitcast.111), kind=kCustom, calls=%fused_computation.clone | custom fusion | bytes 12713984 | tf_op jit(solution)/shard_map/vmap(jit(_take))/gather | solution.py:8
  495.4 161.2 %gather_fusion.2 = bf16[16384,192]{1,0:T(8,128)(2,1)} fusion(bf16[2,2048,192]{2,1,0:T(8,128)(2,1)S(1)} %bitcast.107, s32[16384]{0:T(1024)S(1)} %bitcast.110), kind=kCustom, calls=%fused_computation.1.clone | custom fusion | bytes 12713984 | tf_op jit(solution)/shard_map/vmap(jit(_take))/gather | solution.py:8
  656.6 1.7 copy.37
  658.3 1.7 copy.41
  660.1 1.7 copy.44
  661.8 2.2 copy.47
  664.0 0.0 copy-done.1
  664.0 0.1 compare_bitcast_fusion.3
  664.2 2.2 copy.36
  666.3 2.1 copy.40
  668.5 2.1 copy.43
  670.6 2.2 copy.46
  672.8 79.1 %add_convert_fusion = bf16[2,8192,192]{2,0,1:T(2,128)(2,1)S(1)} fusion(pred[2,8192]{0,1:T(8,128)(4,1)} %copy.46, pred[2,8192]{0,1:T(8,128)(4,1)} %copy.43, pred[2,8192]{0,1:T(8,128)(4,1)} %copy.40, pred[2,8192]{0,1:T(8,128)(4,1)} %copy.36, pred[2,8192]{0,1:T(8,128)(4,1)S(1)} %copy.37, pred[2,8192]{0,1:T(8,128)(4,1)S(1)} %copy.41, ...), kind=kLoop, calls=%fused_computation.5 | loop fusion | flops 50331648 | bytes 31588352 | tf_op jit(solution)/shard_map/convert_element_type | solution.py:42
  751.8 196.1 %all_to_all.18 = bf16[2,8192,192]{2,0,1:T(2,128)(2,1)} all-to-all(bf16[2,8192,192]{2,0,1:T(2,128)(2,1)S(1)} %add_convert_fusion), channel_id=1, replica_groups=mesh['batch'=64,'feat'=4] {'batch'}, dimensions={1} | all-to-all | bytes 12582912 | tf_op jit(solution)/shard_map/all_to_all | solution.py:43
  948.0 20.4 %copy.56 = bf16[2,64,128,192]{2,3,0,1:T(8,128)(2,1)} copy(bf16[2,64,128,192]{3,0,2,1:T(2,128)(2,1)} %bitcast.113) | data formatting | bytes 12582912 | tf_op jit(solution)/shard_map/all_to_all | solution.py:43
  968.4 0.0 all-gather.2.cloned.1.call-update
  968.4 0.2 reduce-scatter.2.cloned.1.call-start
  968.6 0.0 copy-done.3
  968.6 0.1 dynamic-slice_multiply_fusion
  968.7 0.1 copy.34
  968.8 0.1 iota_add_fusion
  968.9 0.1 add.103
  969.0 0.1 compare_and_fusion.4
  969.1 224.3 %all-gather.2.cloned.1.call-done = bf16[512,128,192]{1,2,0:T(8,128)(2,1)} async-done(((bf16[128,128,192]{1,2,0:T(8,128)(2,1)}), bf16[512,128,192]{1,2,0:T(8,128)(2,1)}) %all-gather.2.cloned.1.call-update) | async-done | bytes 25165840 | tf_op jit(solution)/shard_map/all_gather | solution.py:49
  1193.3 18.8 %gather_fusion = bf16[256,128,192]{1,2,0:T(8,128)(2,1)} fusion(bf16[512,128,192]{1,2,0:T(8,128)(2,1)} %all-gather.2.cloned.1.call-done, s32[1024]{0:T(1024)S(1)} %pad_clamp_fusion), kind=kCustom, calls=%fused_computation.4 | custom fusion | bytes 25166848 | tf_op jit(solution)/shard_map/jit(_take)/gather | solution.py:15
  1212.1 27.1 %copy.51 = bf16[4,2,32,128,192]{4,2,3,0,1:T(8,128)(2,1)} copy(bf16[4,2,32,128,192]{3,4,2,1,0:T(8,128)(2,1)} %bitcast.112) | data formatting | bytes 25165824 | tf_op jit(solution)/shard_map/jit(_take)/gather | solution.py:15
  1239.3 14.1 %broadcast_select_fusion.4 = bf16[4,2,32,128,192]{4,2,3,0,1:T(8,128)(2,1)} fusion(bf16[4,2,32,128,192]{4,2,3,0,1:T(8,128)(2,1)} %copy.51, pred[4,2,32]{2,0,1:T(4,128)(4,1)S(1)} %copy.35), kind=kLoop, calls=%fused_computation.10 | loop fusion | flops 6291456 | bytes 25166080 | tf_op jit(solution)/shard_map/jit(_take)/select_n | solution.py:15
  1253.4 11.3 broadcast_multiply_fusion
  1264.7 11.9 fusion.6
  1276.6 0.0 copy-start.2
  1276.6 6.1 convolution_bitcast_fusion
  1282.7 0.0 reduce-scatter.2.cloned.1.call-update
  1282.7 0.7 dynamic_slice.7
  1283.4 32.5 %reduce-scatter.2.cloned.1.call-done = f32[1024,128]{0,1:T(8,128)} async-done(((f32[4096,128]{0,1:T(8,128)}), f32[1024,128]{0,1:T(8,128)}) %reduce-scatter.2.cloned.1.call-update) | async-done | bytes 524304 | tf_op jit(solution)/shard_map/reduce_scatter | solution.py:56
  1315.9 1.2 add_reduce_fusion
  1317.1 8.6 all-reduce
  1325.7 0.0 copy-done.2
  1325.7 2.0 fusion.9
  (11 shorter events, 0.1 us)
Async XLA Ops:
  6.5 1258.2 %copy-start = (bf16[4,32,8]{1,2,0:T(8,128)(2,1)S(1)}, bf16[4,32,8]{1,2,0:T(8,128)(2,1)}, u32[]{:S(2)}) copy-start(bf16[4,32,8]{1,2,0:T(8,128)(2,1)} %param.14) | copy-start | bytes 6148
  6.5 1186.8 %all-gather.2.cloned.1.call-start = ((), (), s32[]{:S(2)}) async-start(), calls=%async_computation.2 | async-start | bytes 31457280 | tf_op jit(solution)/shard_map/all_gather | solution.py:49
  495.4 168.6 %copy-start.1 = (s32[1,2,8192]{2,1,0:T(2,128)S(1)}, s32[1,2,8192]{2,1,0:T(2,128)}, u32[]{:S(2)}) copy-start(s32[1,2,8192]{2,1,0:T(2,128)} %param.12) | copy-start | bytes 196612
  948.0 20.6 %copy-start.3 = (s32[16,2]{0,1:T(2,128)S(1)}, s32[16,2]{0,1:T(2,128)}, u32[]{:S(2)}) copy-start(s32[16,2]{0,1:T(2,128)} %param.13) | copy-start | bytes 388
  968.4 347.6 %reduce-scatter.2.cloned.1.call-start = ((), (), s32[]{:S(2)}) async-start(), calls=%async_computation.3 | async-start | bytes 2621440 | tf_op jit(solution)/shard_map/reduce_scatter | solution.py:56
  1276.6 49.1 %copy-start.2 = (f32[1024]{0:T(1024)S(1)}, f32[1024]{0:T(1024)}, u32[]{:S(2)}) copy-start(f32[1024]{0:T(1024)} %param.17) | copy-start | bytes 12292
Sparse Core Ops, SparseCore 0:
  968.5 224.7 all-gather.1
  1282.8 33.0 reduce-scatter.1
where the time goes:
time: 1340 us; the launch traced here: 1330 us
  local copies, waits for them, and re-layouts  732 us (55%)
  waiting for transfers between devices  257 us (19%)
  blocking collectives  205 us (15%)
  other arithmetic  97.5 us (7%)
  matrix products  29.3 us (2%)
  between operations  13.6 us (1%)
    gather x4, local copies, waits for them, and re-layouts, take_rows(): return jnp.take(table_one, ids_one, axis=0)  645 us
    all_gather x1, waiting for transfers between devices, body(): everything = lax.all_gather(feature_tile, 'feat', axis=0, tiled=True)  224 us
    all_to_all x1, blocking collectives, body(): lax.all_to_all(pooled, 'batch', split_axis=1, concat_axis=0, tiled=True)  196 us
    convert_element_type x1, other arithmetic, body(): pooled = pooled_sum.astype(jnp.bfloat16)  79.1 us
    gather x2, local copies, waits for them, and re-layouts, select_groups(): return jnp.take(source, wanted.reshape(-1), axis=0).reshape(shape_out)  45.9 us
    reduce_scatter x1, waiting for transfers between devices, body(): lax.psum_scatter(lax.dot_general(w_flat, squeezed, (((0,), (1,)), ((), ()...  32.5 us
  transfers between devices with their start and end apart: 2, of which 2 were waited for; matrix products, arithmetic and copies ran while one was open for 0% of the time, Pallas kernels for 0%

commit v1 on v0

--- a/solution.py
+++ b/solution.py
@@ -40,7 +40,10 @@
         live = (own_lengths > slot)[:, :, None]
         pooled_sum = pooled_sum + jnp.where(live, looked.astype(jnp.float32), 0.0)
     pooled = pooled_sum.astype(jnp.bfloat16)
-    feature_tile = lax.all_to_all(pooled, "batch", split_axis=1, concat_axis=0, tiled=True)
+    feature_tile = jnp.concatenate(
+        lax.all_to_all(jnp.stack(jnp.split(pooled, lax.axis_size("batch"), axis=1)), "batch", 0, 0),
+        axis=0,
+    )
     samples = feature_tile.shape[1]
     pair_count = compress.shape[0]
     group_size = compress.shape[1]

time: 1340 us -> 1230 us (0.918)
  other arithmetic: 97.5 us -> 30.3 us
  blocking collectives: 205 us -> 160 us
    convert_element_type x1, other arithmetic: 79.1 us -> 11.9 us  [body(): pooled = pooled_sum.astype(jnp.bfloat16)]
    all_to_all x1, blocking collectives: 196 us -> 151 us  [body(): lax.all_to_all(jnp.stack(jnp.split(pooled, lax.axis_size('batch'), axis=1...]
    gather x4 -> x8, local copies, waits for them, and re-layouts: 645 us -> 685 us  [take_rows(): return jnp.take(table_one, ids_one, axis=0)]
    all_to_all x1 -> x0, local copies, waits for them, and re-layouts: 20.4 us -> none  [body(): lax.all_to_all(pooled, 'batch', split_axis=1, concat_axis=0, tiled=True)]
where the time goes in v1:
time: 1230 us
  local copies, waits for them, and re-layouts  740 us (60%)
  waiting for transfers between devices  256 us (21%)
  blocking collectives  160 us (13%)
  other arithmetic  30.3 us (2%)
  matrix products  29.3 us (2%)
  between operations  13.6 us (1%)
    gather x8, local copies, waits for them, and re-layouts, take_rows(): return jnp.take(table_one, ids_one, axis=0)  685 us
    all_gather x1, waiting for transfers between devices, body(): everything = lax.all_gather(feature_tile, 'feat', axis=0, tiled=True)  224 us
    all_to_all x1, blocking collectives, body(): lax.all_to_all(jnp.stack(jnp.split(pooled, lax.axis_size('batch'), axis=1...  151 us
    gather x2, local copies, waits for them, and re-layouts, select_groups(): return jnp.take(source, wanted.reshape(-1), axis=0).reshape(shape_out)  45.9 us
    reduce_scatter x1, waiting for transfers between devices, body(): lax.psum_scatter(lax.dot_general(w_flat, squeezed, (((0,), (1,)), ((), ()...  32.5 us
  transfers between devices with their start and end apart: 2, of which 2 were waited for; matrix products, arithmetic and copies ran while one was open for 0% of the time, Pallas kernels for 0%

profile of v1, /device:TPU:8, one launch (start us, length us, event | category | flops | bytes accessed | tf_op | source)
XLA Modules:
  0.0 1229.5 jit_solution(1471222722055289580)
XLA Ops:
  6.5 0.0 copy-start
  6.5 0.0 all-gather.2.cloned.1.call-start
  6.5 1.8 fusion.15
  8.3 0.2 fusion.10
  8.5 0.2 compare_and_fusion
  8.7 0.2 fusion.12
  8.9 0.2 compare_and_fusion.2
  9.1 2.7 copy.29
  11.9 161.2 %gather_fusion.1 = bf16[16384,192]{1,0:T(8,128)(2,1)} fusion(bf16[2,2048,192]{2,1,0:T(8,128)(2,1)S(1)} %bitcast.356, s32[16384]{0:T(1024)S(1)} %bitcast.360), kind=kCustom, calls=%fused_computation.clone | custom fusion | bytes 12713984 | tf_op jit(solution)/shard_map/vmap(jit(_take))/gather | solution.py:8
  173.1 10.1 copy.30
  183.2 161.2 %gather_fusion.2 = bf16[16384,192]{1,0:T(8,128)(2,1)} fusion(bf16[2,2048,192]{2,1,0:T(8,128)(2,1)S(1)} %bitcast.357, s32[16384]{0:T(1024)S(1)} %bitcast.362), kind=kCustom, calls=%fused_computation.1.clone | custom fusion | bytes 12713984 | tf_op jit(solution)/shard_map/vmap(jit(_take))/gather | solution.py:8
  344.5 10.1 copy.31
  354.5 161.2 %gather_fusion.3 = bf16[16384,192]{1,0:T(8,128)(2,1)} fusion(bf16[2,2048,192]{2,1,0:T(8,128)(2,1)S(1)} %bitcast.358, s32[16384]{0:T(1024)S(1)} %bitcast.363), kind=kCustom, calls=%fused_computation.2.clone | custom fusion | bytes 12713984 | tf_op jit(solution)/shard_map/vmap(jit(_take))/gather | solution.py:8
  515.7 10.2 copy.32
  525.9 161.2 %gather_fusion.4 = bf16[16384,192]{1,0:T(8,128)(2,1)} fusion(bf16[2,2048,192]{2,1,0:T(8,128)(2,1)S(1)} %bitcast.359, s32[16384]{0:T(1024)S(1)} %bitcast.361), kind=kCustom, calls=%fused_computation.3.clone | custom fusion | bytes 12713984 | tf_op jit(solution)/shard_map/vmap(jit(_take))/gather | solution.py:8
  687.1 0.0 copy-start.1
  687.1 10.1 copy.33
  697.2 0.0 copy-done.1
  697.2 0.1 compare_bitcast_fusion.3
  697.4 11.9 add_convert_fusion
  712.1 151.2 %all_to_all.5 = bf16[64,2,128,192]{2,3,1,0:T(8,128)(2,1)} all-to-all(bf16[64,2,128,192]{2,3,1,0:T(8,128)(2,1)S(1)} %constant_dynamic-update-slice_fusion), channel_id=1, replica_groups=mesh['batch'=64,'feat'=4] {'batch'}, dimensions={0} | all-to-all | bytes 12582912 | tf_op jit(solution)/shard_map/all_to_all | solution.py:44
  863.3 0.0 copy-start.3
  863.3 0.0 all-gather.2.cloned.1.call-update
  863.3 0.2 reduce-scatter.2.cloned.1.call-start
  863.5 0.4 copy-done.3
  864.0 0.1 dynamic-slice_multiply_fusion
  864.0 0.1 copy.27
  864.1 0.1 iota_add_fusion
  864.2 0.1 add.103
  864.3 0.1 compare_and_fusion.4
  864.4 223.9 %all-gather.2.cloned.1.call-done = bf16[512,128,192]{1,2,0:T(8,128)(2,1)} async-done(((bf16[128,128,192]{1,2,0:T(8,128)(2,1)}), bf16[512,128,192]{1,2,0:T(8,128)(2,1)}) %all-gather.2.cloned.1.call-update) | async-done | bytes 25165840 | tf_op jit(solution)/shard_map/all_gather | solution.py:52
  1088.3 18.8 %gather_fusion = bf16[256,128,192]{1,2,0:T(8,128)(2,1)} fusion(bf16[512,128,192]{1,2,0:T(8,128)(2,1)} %all-gather.2.cloned.1.call-done, s32[1024]{0:T(1024)S(1)} %pad_clamp_fusion), kind=kCustom, calls=%fused_computation.4 | custom fusion | bytes 25166848 | tf_op jit(solution)/shard_map/jit(_take)/gather | solution.py:15
  1107.1 27.1 %copy.34 = bf16[4,2,32,128,192]{4,2,3,0,1:T(8,128)(2,1)} copy(bf16[4,2,32,128,192]{3,4,2,1,0:T(8,128)(2,1)} %bitcast.364) | data formatting | bytes 25165824 | tf_op jit(solution)/shard_map/jit(_take)/gather | solution.py:15
  1134.2 14.1 %broadcast_select_fusion = bf16[4,2,32,128,192]{4,2,3,0,1:T(8,128)(2,1)} fusion(bf16[4,2,32,128,192]{4,2,3,0,1:T(8,128)(2,1)} %copy.34, pred[4,2,32]{2,0,1:T(4,128)(4,1)S(1)} %copy.28), kind=kLoop, calls=%fused_computation.5 | loop fusion | flops 6291456 | bytes 25166080 | tf_op jit(solution)/shard_map/jit(_take)/select_n | solution.py:15
  1148.4 11.3 broadcast_multiply_fusion
  1159.7 0.0 copy-done
  1159.7 11.9 fusion.6
  1171.6 0.0 copy-start.2
  1171.6 6.1 convolution_bitcast_fusion
  1177.7 0.0 reduce-scatter.2.cloned.1.call-update
  1177.7 0.7 dynamic_slice.7
  1178.4 32.5 %reduce-scatter.2.cloned.1.call-done = f32[1024,128]{0,1:T(8,128)} async-done(((f32[4096,128]{0,1:T(8,128)}), f32[1024,128]{0,1:T(8,128)}) %reduce-scatter.2.cloned.1.call-update) | async-done | bytes 524304 | tf_op jit(solution)/shard_map/reduce_scatter | solution.py:59
  1210.9 1.2 add_reduce_fusion
  1212.1 8.6 all-reduce
  1220.7 0.0 copy-done.2
  1220.7 2.0 fusion.9
  (72 shorter events, 2.8 us)
Async XLA Ops:
  6.5 1153.2 %copy-start = (bf16[4,32,8]{1,2,0:T(8,128)(2,1)S(1)}, bf16[4,32,8]{1,2,0:T(8,128)(2,1)}, u32[]{:S(2)}) copy-start(bf16[4,32,8]{1,2,0:T(8,128)(2,1)} %param.14) | copy-start | bytes 6148
  6.5 1081.8 %all-gather.2.cloned.1.call-start = ((), (), s32[]{:S(2)}) async-start(), calls=%async_computation.2 | async-start | bytes 31457280 | tf_op jit(solution)/shard_map/all_gather | solution.py:52
  687.1 10.1 copy-start.1
  863.3 0.7 copy-start.3
  863.3 347.6 %reduce-scatter.2.cloned.1.call-start = ((), (), s32[]{:S(2)}) async-start(), calls=%async_computation.3 | async-start | bytes 2621440 | tf_op jit(solution)/shard_map/reduce_scatter | solution.py:59
  1171.6 49.1 %copy-start.2 = (f32[1024]{0:T(1024)S(1)}, f32[1024]{0:T(1024)}, u32[]{:S(2)}) copy-start(f32[1024]{0:T(1024)} %param.17) | copy-start | bytes 12292
Sparse Core Ops, SparseCore 0:
  863.4 224.8 all-gather.1
  1177.8 33.0 reduce-scatter.1
